TPU v7x, 32 devices: a whole 2x2x4 slice. The times are simulated.
32 devices in a mesh: attn: 8 (over z, x), expert: 4 (over y, core).
Axes of the slice: x: 2, y: 2, z: 4, core: 2. Of those that a mesh axis runs over, the one named last changes fastest.
Arguments:
- resid: bfloat16 [512, 6144], P('attn', 'expert')
- query: bfloat16 [512, 6144], P('attn', 'expert'), may hold values from -1 to 1
- key_cache: bfloat16 [512, 8, 128, 128], P('attn', 'expert'), may hold values from -4 to 4
- value_cache: bfloat16 [512, 8, 128, 128], P('attn', 'expert'), may hold values from -6 to 6
- new_key: bfloat16 [512, 1024], P('attn', 'expert'), may hold values from -4 to 4
- new_value: bfloat16 [512, 1024], P('attn', 'expert'), may hold values from -6 to 6
- lengths: int32 [512], P('attn'), may hold values from 1 to 128, as said below
- norm_gain: float32 [6144], P('expert'), may hold values from 0.1 to 1.9
- router_weight: float32 [6144, 8], P('expert'), may hold values from -0.078125 to 0.078125
- expert_ids: int32 [512, 2], P('attn'), may hold values from 0 to 7, as said below
- w_gate: bfloat16 [8, 6144, 8192], P('expert', None, 'attn'), may hold values from -0.078125 to 0.078125
- w_up: bfloat16 [8, 6144, 8192], P('expert', None, 'attn'), may hold values from -0.078125 to 0.078125
- w_down: bfloat16 [8, 8192, 6144], P('expert', 'attn'), may hold values from -0.0625 to 0.0625
Outputs:
- layer_out: bfloat16 [512, 6144], P('attn', 'expert')
Inputs may be any that keep to these rules, and one draw needn't show every extreme that they name: `expert_ids`: each row names two different experts. Within each aligned block of 64 rows (the rows of one index of attn) no expert is named by more than 32 rows, and one expert, the same in every block, is named by exactly 32 rows in each block. `lengths`: some row has all 128 positions filled and some row has one.
All inputs are finite; a program needn't handle non-finite values.
Results may differ from a plain program's by a relative error of at most 0.0095.
Values may be sent and summed in bfloat16 or wider, within the bound.
A program may use at most 128 MiB of HBM per device.

v0:
```python
import math

import jax
import jax.numpy as jnp
from jax import lax
from jax.sharding import PartitionSpec as P

D = 6144
E = 8
CAP = 32


EPSILON = 1e-05


def on_device(
    resid,
    query,
    key_cache,
    value_cache,
    new_key,
    new_value,
    lengths,
    norm_gain,
    router_weight,
    expert_ids,
    w_gate,
    w_up,
    w_down,
):
    row_count = resid.shape[0]
    width_local = resid.shape[1]
    kv_local = key_cache.shape[1]
    cache_slots = key_cache.shape[2]
    head_size = key_cache.shape[3]
    group_size = query.shape[1] // (kv_local * head_size)
    local_experts = w_gate.shape[0]
    expert_devices = lax.axis_size("expert")
    score_scale = 1.0 / math.sqrt(head_size)
    queries = query.reshape(row_count, kv_local, group_size, head_size)
    scores = (
        jnp.einsum("rkgd,rkld->rkgl", queries, key_cache, preferred_element_type=jnp.float32)
        * score_scale
    )
    fresh_score = (
        jnp.einsum(
            "rkgd,rkd->rkg",
            queries,
            new_key.reshape(row_count, kv_local, head_size),
            preferred_element_type=jnp.float32,
        )
        * score_scale
    )
    usable = lax.broadcasted_iota(jnp.int32, (row_count, cache_slots), 1) < lengths[:, None]
    powers = jnp.where(usable[:, None, None, :], jnp.exp(scores), jnp.float32(0.0))
    fresh_power = jnp.exp(fresh_score)
    denominator = jnp.sum(powers, axis=-1) + fresh_power
    weights_cache = (powers / denominator[..., None]).astype(jnp.bfloat16)
    weight_fresh = (fresh_power / denominator).astype(jnp.bfloat16)
    attended = jnp.einsum(
        "rkgl,rkld->rkgd", weights_cache, value_cache, preferred_element_type=jnp.float32
    )
    attended = attended + weight_fresh.astype(jnp.float32)[..., None] * new_value.astype(
        jnp.float32
    ).reshape(row_count, kv_local, 1, head_size)
    hidden_state = resid.astype(jnp.float32) + attended.reshape(row_count, width_local)
    total_square = lax.psum(jnp.sum(hidden_state * hidden_state, axis=1), "expert")
    normed = hidden_state * lax.rsqrt(total_square / D + EPSILON)[:, None] * norm_gain
    logits = lax.psum(jnp.dot(normed, router_weight, precision=lax.Precision.HIGHEST), "expert")
    narrow = normed.astype(jnp.bfloat16)
    choose = expert_ids[:, :, None] == lax.broadcasted_iota(jnp.int32, (1, 1, E), 2)
    picked = jnp.sum(jnp.where(choose, logits[:, None, :], jnp.float32(0.0)), axis=2)
    first_weight = 1.0 / (1.0 + jnp.exp(picked[:, 1] - picked[:, 0]))
    second_weight = 1.0 / (1.0 + jnp.exp(picked[:, 0] - picked[:, 1]))
    hits = jnp.sum(choose.astype(jnp.int32), axis=1)
    before = jnp.cumsum(hits, axis=0) - hits
    slot_index = jnp.sum(jnp.where(choose, before[:, None, :], 0), axis=2)
    slot_match = slot_index[:, :, None] == lax.broadcasted_iota(jnp.int32, (1, 1, CAP), 2)
    selector = jnp.einsum(
        "rke,rkc->ecr",
        choose.astype(jnp.bfloat16),
        slot_match.astype(jnp.bfloat16),
        preferred_element_type=jnp.float32,
    ).astype(jnp.bfloat16)
    whole_rows = lax.all_gather(narrow, "expert", axis=1, tiled=True)
    own_selector = lax.dynamic_slice_in_dim(
        selector, lax.axis_index("expert") * local_experts, local_experts, 0
    )
    outgoing = jnp.einsum(
        "ecr,rd->ecd", own_selector, whole_rows, preferred_element_type=jnp.float32
    ).astype(jnp.bfloat16)
    slab_rows = lax.all_gather(outgoing, "attn", axis=1, tiled=True)
    gate_part = jnp.einsum("end,edf->enf", slab_rows, w_gate, preferred_element_type=jnp.float32)
    up_part = jnp.einsum("end,edf->enf", slab_rows, w_up, preferred_element_type=jnp.float32)
    activation = (jax.nn.silu(gate_part) * up_part).astype(jnp.bfloat16)
    summed = lax.psum_scatter(
        jnp.einsum("enf,efd->ned", activation, w_down, preferred_element_type=jnp.float32).astype(
            jnp.bfloat16
        ),
        "attn",
        scatter_dimension=0,
        tiled=True,
    )
    expert_result = summed
    expert_result = expert_result.reshape(CAP, local_experts, expert_devices, width_local)
    returned = lax.all_to_all(expert_result, "expert", split_axis=2, concat_axis=1, tiled=True)
    flat_result = returned.reshape(CAP * E, width_local)
    target_index = slot_index * E + expert_ids
    picker = (
        target_index[:, :, None] == lax.broadcasted_iota(jnp.int32, (1, 1, CAP * E), 2)
    ).astype(jnp.bfloat16)
    taken = jnp.einsum("rkm,md->krd", picker, flat_result, preferred_element_type=jnp.float32)
    total = hidden_state + first_weight[:, None] * taken[0] + second_weight[:, None] * taken[1]
    return total.astype(jnp.bfloat16)


def solution(mesh):
    return jax.shard_map(
        on_device,
        mesh=mesh,
        in_specs=(
            P("attn", "expert"),
            P("attn", "expert"),
            P("attn", "expert", None, None),
            P("attn", "expert", None, None),
            P("attn", "expert"),
            P("attn", "expert"),
            P("attn"),
            P("expert"),
            P("expert", None),
            P("attn", None),
            P("expert", None, "attn"),
            P("expert", None, "attn"),
            P("expert", "attn", None),
        ),
        out_specs=P("attn", "expert"),
        check_vma=False,
    )
```

profile of v0, /device:TPU:16, one launch (start us, length us, event | category | flops | bytes accessed | tf_op | source)
XLA Modules:
  0.0 322.0 jit_solution(12968321372887208241)
XLA Ops:
  6.5 0.7 iota_compare_fusion.4
  7.3 0.8 copy.40
  8.1 0.2 convert_reduce_fusion
  8.3 1.2 select_reduce_fusion
  9.6 0.8 reshape.61
  10.4 0.8 reshape.55
  11.2 0.4 fusion.14
  11.6 1.2 reshape.50
  12.8 0.3 fusion.26
  13.0 4.6 %fusion.25 = (f32[64,2,6]{2,1,0:T(2,128)S(1)}, f32[64,2,6,128]{3,2,1,0:T(8,128)S(1)}) fusion(bf16[64,2,6,128]{3,2,1,0:T(8,128)(2,1)S(1)} %reshape.50, bf16[64,2,128,128]{3,2,1,0:T(8,128)(2,1)} %param.15, pred[64,128]{1,0:T(8,128)(4,1)S(1)} %iota_compare_fusion.4), kind=kOutput, calls=%fused_computation.51 | convolution fusion | flops 25459968 | bytes 4795392 | tf_op jit(solution)/shard_map/rkgd,rkld->rkgl/dot_general | solution.py:42
  17.8 3.4 %convolution_add_fusion = f32[64,2,6,128]{3,2,1,0:T(8,128)S(1)} fusion(bf16[64,2,128,128]{3,2,1,0:T(8,128)(2,1)} %param.16, f32[64,2,6,128]{3,2,1,0:T(8,128)S(1)} %get-tuple-element.12, f32[64,2,128]{2,1,0:T(2,128)S(1)} %reshape.55, f32[64,2,6]{2,1,0:T(2,128)S(1)} %get-tuple-element.6, f32[64,2,6]{2,1,0:T(2,128)S(1)} %get-tuple-element.5), kind=kOutput, calls=%fused_computation.5 | convolution fusion | flops 25559040 | bytes 5052416 | tf_op jit(solution)/shard_map/rkgl,rkld->rkgd/dot_general | solution.py:60
  21.3 0.2 multiply_reduce_fusion
  21.5 6.9 %psum.14 = f32[64]{0:T(128)S(1)} all-reduce(f32[64]{0:T(128)S(1)} %multiply_reduce_fusion), channel_id=1, replica_groups=mesh['attn'=8,'expert'=4] {'expert'}, use_global_device_ids=true, to_apply=%region_2.3 | all-reduce | flops 64 | bytes 512 | tf_op jit(solution)/shard_map/psum | solution.py:67
  28.4 0.1 fusion.9
  28.5 7.6 %all_gather.6 = bf16[64,6144]{1,0:T(8,128)(2,1)S(1)} all-gather(bf16[64,1536]{1,0:T(8,128)(2,1)S(1)} %fusion.9), channel_id=1, replica_groups=mesh['attn'=8,'expert'=4] {'expert'}, dimensions={1}, use_global_device_ids=true | all-gather | bytes 983040 | tf_op jit(solution)/shard_map/all_gather | solution.py:85
  36.1 1.3 convolution_convert_fusion.1
  37.5 0.2 reduce-scatter.2.cloned.1.call-start
  37.7 98.8 %all-gather.2.cloned.1.call-done = bf16[2,256,6144]{2,1,0:T(8,128)(2,1)} async-done(((bf16[2,32,6144]{2,1,0:T(8,128)(2,1)}), bf16[2,256,6144]{2,1,0:T(8,128)(2,1)}) %all-gather.2.cloned.1.call-update) | async-done | bytes 6291472 | tf_op jit(solution)/shard_map/all_gather | solution.py:92
  136.5 13.5 %fusion.27 = f32[2,256,1024]{2,1,0:T(8,128)S(1)} fusion(bf16[2,256,6144]{2,1,0:T(8,128)(2,1)} %all-gather.2.cloned.1.call-done, bf16[2,6144,1024]{2,1,0:T(8,128)(2,1)} %param.23), kind=kOutput, calls=%fused_computation.53 | convolution fusion | flops 6442450944 | bytes 33554432 | tf_op jit(solution)/shard_map/end,edf->enf/dot_general | solution.py:93
  150.1 12.3 %multiply_convert_fusion = bf16[2,256,1024]{2,1,0:T(8,128)(2,1)S(1)} fusion(f32[2,256,1024]{2,1,0:T(8,128)S(1)} %fusion.27, bf16[2,256,6144]{2,1,0:T(8,128)(2,1)S(1)} %copy-done.4, bf16[2,6144,1024]{2,1,0:T(8,128)(2,1)} %param.24), kind=kOutput, calls=%fused_computation.4 | convolution fusion | flops 6445596672 | bytes 34603008 | tf_op jit(solution)/shard_map/end,edf->enf/dot_general | solution.py:94
  162.4 16.8 %fusion = bf16[256,2,6144]{2,0,1:T(8,128)(2,1)} fusion(bf16[2,256,1024]{2,1,0:T(8,128)(2,1)S(1)} %multiply_convert_fusion, bf16[2,1024,6144]{2,1,0:T(8,128)(2,1)} %param.25), kind=kOutput, calls=%fused_computation.1 | convolution fusion | flops 6445596672 | bytes 32505856 | tf_op jit(solution)/shard_map/enf,efd->ned/dot_general | solution.py:97
  179.3 0.5 fusion.10
  179.8 5.8 %psum.15 = f32[64,8]{0,1:T(8,128)S(1)} all-reduce(f32[64,8]{0,1:T(8,128)S(1)} %fusion.10), channel_id=1, replica_groups=mesh['attn'=8,'expert'=4] {'expert'}, use_global_device_ids=true, to_apply=%region_3.4 | all-reduce | flops 512 | bytes 4096 | tf_op jit(solution)/shard_map/psum | solution.py:69
  185.7 0.2 select_reduce_fusion.1
  185.9 109.8 %reduce-scatter.2.cloned.1.call-done = bf16[32,2,6144]{2,0,1:T(8,128)(2,1)} async-done(((bf16[256,2,6144]{2,0,1:T(8,128)(2,1)}), bf16[32,2,6144]{2,0,1:T(8,128)(2,1)}) %reduce-scatter.2.cloned.1.call-update) | async-done | bytes 786448 | tf_op jit(solution)/shard_map/reduce_scatter | solution.py:96
  295.7 2.1 copy.56
  297.8 3.5 %all-to-all-start = ((bf16[32,2,4,1536]{3,0,1,2:T(8,128)(2,1)}), bf16[32,2,4,1536]{3,0,1,2:T(8,128)(2,1)S(1)}, u32[]{:S(2)}, u32[]{:S(2)}) async-start(bf16[32,2,4,1536]{3,0,1,2:T(8,128)(2,1)} %bitcast.52), calls=%async_computation.1 | async-start | bytes 1572864 | tf_op jit(solution)/shard_map/all_to_all | solution.py:106
  301.6 11.3 %all-to-all-done = bf16[32,2,4,1536]{3,0,1,2:T(8,128)(2,1)S(1)} async-done(((bf16[32,2,4,1536]{3,0,1,2:T(8,128)(2,1)}), bf16[32,2,4,1536]{3,0,1,2:T(8,128)(2,1)S(1)}, u32[]{:S(2)}, u32[]{:S(2)}) %all-to-all-start) | async-done | bytes 786464 | tf_op jit(solution)/shard_map/all_to_all | solution.py:106
  312.9 0.8 copy.46
  313.7 0.3 reshape.59
  314.0 0.3 convolution_bitcast_fusion
  314.3 0.8 fusion.6
  (26 shorter events, 0.8 us)
Async XLA Ops:
  6.5 172.7 %copy-start = (f32[1536,8]{0,1:T(8,128)S(1)}, f32[1536,8]{0,1:T(8,128)}, u32[]{:S(2)}) copy-start(f32[1536,8]{0,1:T(8,128)} %param.21) | copy-start | bytes 147460
  6.5 130.0 %all-gather.2.cloned.1.call-start = ((), (), s32[]{:S(2)}) async-start(), calls=%async_computation.2 | async-start | bytes 7077888 | tf_op jit(solution)/shard_map/all_gather | solution.py:92
  13.0 8.3 %copy-start.1 = (bf16[64,1536]{1,0:T(8,128)(2,1)S(1)}, bf16[64,1536]{1,0:T(8,128)(2,1)}, u32[]{:S(2)}) copy-start(bf16[64,1536]{1,0:T(8,128)(2,1)} %param.13) | copy-start | bytes 589828
  17.7 10.8 %copy-start.2 = (f32[1536]{0:T(1024)S(1)}, f32[1536]{0:T(1024)}, u32[]{:S(2)}) copy-start(f32[1536]{0:T(1024)} %param.20) | copy-start | bytes 18436
  37.5 258.3 %reduce-scatter.2.cloned.1.call-start = ((), (), s32[]{:S(2)}) async-start(), calls=%async_computation.3 | async-start | bytes 7077888 | tf_op jit(solution)/shard_map/reduce_scatter | solution.py:96
  136.5 13.6 %copy-start.4 = (bf16[2,256,6144]{2,1,0:T(8,128)(2,1)S(1)}, bf16[2,256,6144]{2,1,0:T(8,128)(2,1)}, u32[]{:S(2)}) copy-start(bf16[2,256,6144]{2,1,0:T(8,128)(2,1)} %all-gather.2.cloned.1.call-done) | copy-start | bytes 18874372
  179.2 122.4 %copy-start.3 = (s32[64,2]{0,1:T(2,128)S(1)}, s32[64,2]{0,1:T(2,128)}, u32[]{:S(2)}) copy-start(s32[64,2]{0,1:T(2,128)} %param.22) | copy-start | bytes 1540
  297.8 15.1 %all-to-all-start = ((bf16[32,2,4,1536]{3,0,1,2:T(8,128)(2,1)}), bf16[32,2,4,1536]{3,0,1,2:T(8,128)(2,1)S(1)}, u32[]{:S(2)}, u32[]{:S(2)}) async-start(bf16[32,2,4,1536]{3,0,1,2:T(8,128)(2,1)} %bitcast.52), calls=%async_computation.1 | async-start | bytes 1572864 | tf_op jit(solution)/shard_map/all_to_all | solution.py:106
Sparse Core Ops, SparseCore 0:
  37.6 98.8 all-gather.1
  179.3 116.3 reduce-scatter.1
where the time goes:
time: 325 us; the launch traced here: 322 us
  waiting for transfers between devices  220 us (68%)
  matrix products  53.5 us (16%)
  blocking collectives  20.3 us (6%)
  between operations  13.6 us (4%)
  local copies, waits for them, and re-layouts  7.22 us (2%)
  starting transfers between devices  3.72 us (1%)
  other arithmetic  3.66 us (1%)
    reduce_scatter x1, waiting for transfers between devices, on_device(): lax.psum_scatter(jnp.einsum('enf,efd->ned', activation, w_down, preferred...  110 us
    all_gather x1, waiting for transfers between devices, on_device(): slab_rows = lax.all_gather(outgoing, 'attn', axis=1, tiled=True)  98.8 us
    dot_general x1, matrix products, on_device(): jnp.einsum('enf,efd->ned', activation, w_down, preferred_element_type=jnp...  16.8 us
    dot_general x1, matrix products, on_device(): jnp.einsum('end,edf->enf', slab_rows, w_gate, preferred_element_type=jnp....  13.5 us
    dot_general x1, matrix products, on_device(): jnp.einsum('end,edf->enf', slab_rows, w_up, preferred_element_type=jnp.fl...  12.3 us
    all_to_all x1, waiting for transfers between devices, on_device(): lax.all_to_all(expert_result, 'expert', split_axis=2, concat_axis=1, tile...  11.3 us
    all_gather x1, blocking collectives, on_device(): whole_rows = lax.all_gather(narrow, 'expert', axis=1, tiled=True)  7.56 us
    psum x1, blocking collectives, on_device(): lax.psum(jnp.sum(hidden_state * hidden_state, axis=1), 'expert')  6.93 us
  transfers between devices with their start and end apart: 3, of which 3 were waited for; matrix products, arithmetic and copies ran while one was open for 0% of the time, Pallas kernels for 0%

commit v1 on v0

v1 whole, which is shorter than its diff:
```python
import functools
import math

import jax
import jax.numpy as jnp
from jax import lax
from jax.experimental import pallas as pl
from jax.experimental.pallas import tpu as pltpu
from jax.sharding import PartitionSpec as P

EPSILON = 1e-05
LANES = 128
CORES = 2
PARTS = 3
STAT = 16
MESH = pl.DeviceIdType.MESH


def grid_of(attn, expert):
    ny = max(expert // CORES, 1)
    nx = ny if attn % ny == 0 else 1
    return attn // nx, nx, ny


def halves_of(width):
    tiles = width // LANES
    first = (tiles - tiles // 2) * LANES
    return pl.ds(0, first), pl.ds(first, width - first)


class Place:
    def __init__(self, sizes):
        self.nz, self.nx, self.ny = sizes
        a = lax.axis_index("attn")
        e = lax.axis_index("expert")
        self.z, self.x = a // self.nx, lax.rem(a, self.nx)
        self.y, self.c = e // CORES, lax.rem(e, CORES)

    def device(self, z=None, x=None, y=None, c=None):
        z = self.z if z is None else z
        x = self.x if x is None else x
        y = self.y if y is None else y
        c = self.c if c is None else c
        return (z * self.nx + x, y * CORES + c)

    def greet(self):
        barrier = pltpu.get_barrier_semaphore()
        count = jnp.int32(1)

        def signal(dev):
            pl.semaphore_signal(barrier, inc=1, device_id=dev, device_id_type=MESH)

        signal(self.device(c=1 - self.c))
        for name, p, n in (("z", self.z, self.nz), ("x", self.x, self.nx), ("y", self.y, self.ny)):
            for step in (-1, 1):
                inside = jnp.logical_and(p + step >= 0, p + step < n)
                pl.when(inside)(functools.partial(signal, self.device(**{name: p + step})))
                count = count + inside.astype(jnp.int32)
        pl.semaphore_wait(barrier, count)


def gather_kernel(sizes, x_ref, g_ref, local_sem, z_send, z_recv, p1_send, p1_recv, p2_send, p2_recv, s_send, s_recv):
    me = Place(sizes)
    nz, nx, ny = sizes
    z, x, y, c = me.z, me.x, me.y, me.c
    width = x_ref.shape[1]
    cols = halves_of(width)
    me.greet()
    started = []

    def send(cond, src, dst, ssem, rsem, dev):
        copy = pltpu.make_async_remote_copy(
            src_ref=src, dst_ref=dst, send_sem=ssem, recv_sem=rsem, device_id=dev, device_id_type=MESH
        )
        started.append((cond, copy))
        if cond is None:
            copy.start()
        else:
            pl.when(cond)(copy.start)

    def await_block(dst, ssem, rsem):
        pltpu.make_async_remote_copy(
            src_ref=dst, dst_ref=dst, send_sem=ssem, recv_sem=rsem,
            device_id=me.device(c=1 - c), device_id_type=MESH,
        ).wait_recv()

    def block(bz, bx, by, core=None):
        core = c if core is None else core
        return g_ref.at[bz * nx + bx, by * CORES + core]

    def half(ref, h):
        return ref.at[:, cols[h]]

    def to_sibling(cond, src, bz, bx, by, h):
        slot = (bz * nx + bx, by, h)
        send(cond, half(src, h), half(block(bz, bx, by), h), s_send.at[slot], s_recv.at[slot], me.device(c=1 - c))

    def line(h, stage):
        return ("x", x, nx) if (h == 0) == (stage == 0) else ("y", y, ny)

    def along(cond, src, dst, h, stage, step, way, slot):
        name, p, n = line(h, stage)
        to = p + 1 if way == 0 else p - 1
        inside = to < n if way == 0 else to >= 0
        ssem, rsem = (p1_send, p1_recv) if stage == 0 else (p2_send, p2_recv)
        index = (h, step, way) + slot
        cond = inside if cond is None else jnp.logical_and(cond, inside)
        send(cond, half(src, h), half(dst, h), ssem.at[index], rsem.at[index], me.device(**{name: to}))

    def spread(cond, src, bz):
        for h in range(2):
            for way in range(2):
                along(cond, src, block(bz, x, y), h, 0, 0, way, (bz,))
            to_sibling(cond, src, bz, x, y, h)

    def z_hop(cond, src, bz, step, way):
        to = z + 1 if way == 0 else z - 1
        inside = to < nz if way == 0 else to >= 0
        cond = inside if cond is None else jnp.logical_and(cond, inside)
        send(cond, src, block(bz, x, y), z_send.at[step, way], z_recv.at[step, way], me.device(z=to))

    for way in range(2):
        if nz > 1:
            z_hop(None, x_ref, z, 0, way)
    spread(None, x_ref, z)
    local = pltpu.make_async_copy(x_ref, block(z, x, y), local_sem)
    local.start()
    for step in range(1, nz):
        for way in range(2):
            bz = z - step if way == 0 else z + step
            have = bz >= 0 if way == 0 else bz < nz
            dst = block(bz, x, y)
            pl.when(have)(functools.partial(await_block, dst, z_send.at[step - 1, way], z_recv.at[step - 1, way]))
            if step < nz - 1:
                z_hop(have, dst, bz, step, way)
            spread(have, dst, bz)
    turn = jnp.where(z < nz // 2, 1, nz - 1)
    order = [lax.rem(z + k * turn, nz) for k in range(nz)]

    def second(cond, src, h, bz, other):
        for way in range(2):
            along(cond, src, src, h, 1, 0, way, (bz, other))

    local.wait()
    for bz in order:
        for h in range(2):
            second(None, block(bz, x, y), h, bz, line(h, 0)[1])
    for step in range(1, max(nx, ny)):
        for bz in order:
            for h in range(2):
                name, p, n = line(h, 0)
                if step >= n:
                    continue
                for way in range(2):
                    q = p - step if way == 0 else p + step
                    have = q >= 0 if way == 0 else q < n
                    bx, by = (q, y) if name == "x" else (x, q)
                    dst = block(bz, bx, by)
                    index = (h, step - 1, way, bz)
                    pl.when(have)(functools.partial(await_block, half(dst, h), p1_send.at[index], p1_recv.at[index]))
                    if step < n - 1:
                        along(have, dst, dst, h, 0, step, way, (bz,))
                    second(have, dst, h, bz, q)
                    to_sibling(have, dst, bz, bx, by, h)
    for step in range(1, max(nx, ny)):
        for k in range(max(nx, ny)):
            for bz in order:
                for h in range(2):
                    _, first_p, first_n = line(h, 0)
                    name, p, n = line(h, 1)
                    if step >= n or k >= first_n:
                        continue
                    other = lax.rem(first_p + k, first_n)
                    for way in range(2):
                        q = p - step if way == 0 else p + step
                        have = q >= 0 if way == 0 else q < n
                        bx, by = (q, other) if name == "x" else (other, q)
                        dst = block(bz, bx, by)
                        index = (h, step - 1, way, bz, other)
                        pl.when(have)(
                            functools.partial(await_block, half(dst, h), p2_send.at[index], p2_recv.at[index])
                        )
                        if step < n - 1:
                            along(have, dst, dst, h, 1, step, way, (bz, other))
                        to_sibling(have, dst, bz, bx, by, h)
    for bz in range(nz):
        for bx in range(nx):
            for by in range(ny):
                for h in range(2):
                    slot = (bz * nx + bx, by, h)
                    await_block(half(block(bz, bx, by, 1 - c), h), s_send.at[slot], s_recv.at[slot])
    for cond, copy in started:
        if cond is None:
            copy.wait_send()
        else:
            pl.when(cond)(copy.wait_send)


def gather_all(block, sizes):
    nz, nx, ny = sizes
    rows, width = block.shape
    wide = max(nx, ny)
    steps = max(wide - 1, 1)
    dma = pltpu.SemaphoreType.DMA
    stage = [dma((max(nz - 1, 1), 2))] * 2 + [dma((2, steps, 2, nz))] * 2
    stage += [dma((2, steps, 2, nz, wide))] * 2 + [dma((nz * nx, ny, 2))] * 2
    return pl.pallas_call(
        functools.partial(gather_kernel, sizes),
        out_shape=jax.ShapeDtypeStruct((nz * nx, ny * CORES, rows, width), block.dtype),
        in_specs=[pl.BlockSpec(memory_space=pltpu.VMEM)],
        out_specs=pl.BlockSpec(memory_space=pl.ANY),
        scratch_shapes=[dma] + stage,
        compiler_params=pltpu.CompilerParams(collective_id=0, has_side_effects=True),
        name="gather_all",
    )(block)


def reduce_kernel(
    sizes, p_ref, o_ref, acc, sib, r1, r2, r3, s_send, s_recv, c1_send, c1_recv, c2_send, c2_recv, c3_send, c3_recv
):
    me = Place(sizes)
    nz, nx, ny = sizes
    z, x, y, c = me.z, me.x, me.y, me.c
    width = o_ref.shape[1]
    cols = halves_of(width)
    whole = (pl.ds(0, width),)
    me.greet()
    started = []

    def remote(src, dst, ssem, rsem, dev):
        return pltpu.make_async_remote_copy(
            src_ref=src, dst_ref=dst, send_sem=ssem, recv_sem=rsem, device_id=dev, device_id_type=MESH
        )

    def part(by, core):
        return pl.ds(pl.multiple_of((by * CORES + core) * width, LANES), width)

    blocks = [(bz, bx, by) for bz in range(nz) for bx in range(nx) for by in range(ny)]
    for bz, bx, by in blocks:
        a = bz * nx + bx
        copy = remote(
            p_ref.at[a, :, part(by, 1 - c)], sib.at[a, by], s_send.at[a, by], s_recv.at[a, by], me.device(c=1 - c)
        )
        copy.start()
        started.append((None, copy))

    def add(view, col, from_ref):
        view[:, col] = (view[:, col].astype(jnp.float32) + from_ref[:, col].astype(jnp.float32)).astype(view.dtype)

    def receive(view, col, landing, way, ssem, rsem):
        remote(landing[way].at[:, col], landing[way].at[:, col], ssem.at[way], rsem.at[way], me.device(c=1 - c)).wait_recv()
        add(view, col, landing[way])

    def chain(view, col, name, target, landing, ssem, rsem, here=None):
        p, n = {"x": (x, nx), "y": (y, ny), "z": (z, nz)}[name]
        for way in range(2):
            to = p + 1 if way == 0 else p - 1
            go = p < target if way == 0 else p > target
            if here is not None:
                go = jnp.logical_and(here, go)
            inner = p > 0 if way == 0 else p < n - 1
            if n > 2:
                pl.when(jnp.logical_and(go, inner))(
                    functools.partial(receive, view, col, landing, way, ssem, rsem)
                )
            copy = remote(
                view.at[:, col], landing[way].at[:, col], ssem.at[way], rsem.at[way], me.device(**{name: to})
            )
            pl.when(go)(copy.start)
            started.append((go, copy))

    def finish(here, view, col, name, landing, ssem, rsem):
        p, n = {"x": (x, nx), "y": (y, ny), "z": (z, nz)}[name]
        for way in range(2):
            cond = p > 0 if way == 0 else p < n - 1
            cond = jnp.logical_and(here, cond)
            pl.when(cond)(functools.partial(receive, view, col, landing, way, ssem, rsem))

    def lines(h, bx, by):
        first, last = (("y", by), ("x", bx)) if h == 0 else (("x", bx), ("y", by))
        return first, last

    def first_args(h, a, by):
        return [r1.at[way, a, by] for way in range(2)], c1_send.at[h, a, by], c1_recv.at[h, a, by]

    def second_args(h, bz, bx, by):
        k = bz * max(nx, ny) + (bx if h == 0 else by)
        return [r2.at[way, k] for way in range(2)], c2_send.at[h, k], c2_recv.at[h, k]

    at = {"x": x, "y": y}
    for bz, bx, by in blocks:
        a = bz * nx + bx
        remote(sib.at[a, by], sib.at[a, by], s_send.at[a, by], s_recv.at[a, by], me.device(c=1 - c)).wait_recv()
        acc[a, by] = (
            p_ref[a, :, part(by, c)].astype(jnp.float32) + sib[a, by].astype(jnp.float32)
        ).astype(acc.dtype)
        for h in range(2):
            (name, target), _ = lines(h, bx, by)
            chain(acc.at[a, by], cols[h], name, target, *first_args(h, a, by))
    for bz, bx, by in blocks:
        a = bz * nx + bx
        for h in range(2):
            (name, target), (name2, target2) = lines(h, bx, by)
            here = at[name] == target
            finish(here, acc.at[a, by], cols[h], name, *first_args(h, a, by))
            chain(acc.at[a, by], cols[h], name2, target2, *second_args(h, bz, bx, by), here=here)
    for bz, bx, by in blocks:
        a = bz * nx + bx
        here = jnp.logical_and(x == bx, y == by)
        for h in range(2):
            _, (name2, target2) = lines(h, bx, by)
            finish(here, acc.at[a, by], cols[h], name2, *second_args(h, bz, bx, by))
    for bz in sorted(range(nz), key=lambda place: min(place, nz - 1 - place)):
        view = acc.at[bz * nx + x, y]
        landing = [r3.at[way, bz] for way in range(2)]
        chain(view, whole[0], "z", bz, landing, c3_send.at[bz], c3_recv.at[bz])
    for bz in range(nz):
        landing = [r3.at[way, bz] for way in range(2)]

        @pl.when(z == bz)
        def _():
            total = acc[bz * nx + x, y].astype(jnp.float32)
            o_ref[...] = total

        for way in range(2):
            cond = jnp.logical_and(z == bz, z > 0 if way == 0 else z < nz - 1)

            @pl.when(cond)
            def _():
                remote(
                    landing[way], landing[way], c3_send.at[bz, way], c3_recv.at[bz, way], me.device(c=1 - c)
                ).wait_recv()
                o_ref[...] += landing[way][...].astype(jnp.float32)

    for cond, copy in started:
        if cond is None:
            copy.wait_send()
        else:
            pl.when(cond)(copy.wait_send)


def reduce_all(partial, sizes):
    nz, nx, ny = sizes
    attn, rows, full = partial.shape
    width = full // (ny * CORES)
    wide = max(nx, ny)
    dma = pltpu.SemaphoreType.DMA
    kind = partial.dtype
    return pl.pallas_call(
        functools.partial(reduce_kernel, sizes),
        out_shape=jax.ShapeDtypeStruct((rows, width), jnp.float32),
        in_specs=[pl.BlockSpec(memory_space=pltpu.VMEM)],
        out_specs=pl.BlockSpec(memory_space=pltpu.VMEM),
        scratch_shapes=[
            pltpu.VMEM((attn, ny, rows, width), kind),
            pltpu.VMEM((attn, ny, rows, width), kind),
            pltpu.VMEM((2, attn, ny, rows, width), kind),
            pltpu.VMEM((2, nz * wide, rows, width), kind),
            pltpu.VMEM((2, nz, rows, width), kind),
        ]
        + [dma((attn, ny))] * 2
        + [dma((2, attn, ny, 2))] * 2
        + [dma((2, nz * wide, 2))] * 2
        + [dma((nz, 2))] * 2,
        compiler_params=pltpu.CompilerParams(
            collective_id=1, has_side_effects=True, vmem_limit_bytes=60 * 2**20
        ),
        name="reduce_all",
    )(partial)


def pick_kernel(sel_ref, g_ref, out_ref):
    local, cap, rows = sel_ref.shape[1:]
    devices = g_ref.shape[1]
    width = out_ref.shape[2] // devices
    chosen = sel_ref[0].reshape(local * cap, rows)
    for e in range(devices):
        taken = jnp.dot(chosen, g_ref[0, e, :, :width], preferred_element_type=jnp.float32)
        taken = taken.astype(out_ref.dtype).reshape(local, cap, width)
        out_ref[:, :, e * width : (e + 1) * width] = taken


def pick_rows(selector, gathered, width):
    attn, local, cap, rows = selector.shape
    devices, full = gathered.shape[1], gathered.shape[3]
    return pl.pallas_call(
        pick_kernel,
        grid=(attn,),
        out_shape=jax.ShapeDtypeStruct((local, attn * cap, devices * width), gathered.dtype),
        in_specs=[
            pl.BlockSpec((1, local, cap, rows), lambda a: (a, 0, 0, 0)),
            pl.BlockSpec((1, devices, rows, full), lambda a: (a, 0, 0, 0)),
        ],
        out_specs=pl.BlockSpec((local, cap, devices * width), lambda a: (0, a, 0)),
        name="pick_rows",
    )(selector, gathered)


def place_kernel(sel_ref, y_ref, out_ref):
    local = sel_ref.shape[1]
    total = None
    for n in range(local):
        term = lax.dot_general(
            sel_ref[0, n], y_ref[n], (((0,), (0,)), ((), ())), preferred_element_type=jnp.float32
        )
        total = term if total is None else total + term
    out_ref[0] = total.astype(out_ref.dtype)


def place_rows(selector, outputs):
    attn, local, cap, rows = selector.shape
    full = outputs.shape[2]
    return pl.pallas_call(
        place_kernel,
        grid=(attn,),
        out_shape=jax.ShapeDtypeStruct((attn, rows, full), jnp.bfloat16),
        in_specs=[
            pl.BlockSpec((1, local, cap, rows), lambda a: (a, 0, 0, 0)),
            pl.BlockSpec((local, cap, full), lambda a: (0, a, 0)),
        ],
        out_specs=pl.BlockSpec((1, rows, full), lambda a: (a, 0, 0)),
        name="place_rows",
    )(selector, outputs)


def on_device(
    sizes,
    resid,
    query,
    key_cache,
    value_cache,
    new_key,
    new_value,
    lengths,
    norm_gain,
    router_weight,
    expert_ids,
    w_gate,
    w_up,
    w_down,
):
    row_count, width_local = resid.shape
    kv_local, cache_slots, head_size = key_cache.shape[1:]
    group_size = query.shape[1] // (kv_local * head_size)
    local_experts, features, _ = w_gate.shape
    experts = router_weight.shape[1]
    cap = row_count // 2
    score_scale = 1.0 / math.sqrt(head_size)
    queries = query.reshape(row_count, kv_local, group_size, head_size)
    scores = (
        jnp.einsum("rkgd,rkld->rkgl", queries, key_cache, preferred_element_type=jnp.float32) * score_scale
    )
    fresh_score = (
        jnp.einsum(
            "rkgd,rkd->rkg",
            queries,
            new_key.reshape(row_count, kv_local, head_size),
            preferred_element_type=jnp.float32,
        )
        * score_scale
    )
    usable = lax.broadcasted_iota(jnp.int32, (row_count, cache_slots), 1) < lengths[:, None]
    powers = jnp.where(usable[:, None, None, :], jnp.exp(scores), jnp.float32(0.0))
    fresh_power = jnp.exp(fresh_score)
    denominator = jnp.sum(powers, axis=-1) + fresh_power
    weights_cache = (powers / denominator[..., None]).astype(jnp.bfloat16)
    weight_fresh = (fresh_power / denominator).astype(jnp.bfloat16)
    attended = jnp.einsum(
        "rkgl,rkld->rkgd", weights_cache, value_cache, preferred_element_type=jnp.float32
    )
    attended = attended + weight_fresh.astype(jnp.float32)[..., None] * new_value.astype(
        jnp.float32
    ).reshape(row_count, kv_local, 1, head_size)
    hidden_state = resid.astype(jnp.float32) + attended.reshape(row_count, width_local)
    gained = hidden_state * norm_gain
    square = jnp.sum(hidden_state * hidden_state, axis=1, keepdims=True)
    raw_logits = jnp.dot(gained, router_weight, precision=lax.Precision.HIGHEST)
    stats = jnp.concatenate([raw_logits, square], axis=1)
    pieces, rest = [], jnp.pad(stats, ((0, 0), (0, STAT - experts - 1)))
    for _ in range(PARTS):
        piece = lax.reduce_precision(rest, 8, 7)
        pieces.append(piece)
        rest = rest - piece
    pieces.append(expert_ids.astype(jnp.float32))
    packed = jnp.concatenate(pieces, axis=1)
    packed = jnp.pad(packed, ((0, 0), (0, LANES - packed.shape[1])))
    block = jnp.concatenate([gained, packed], axis=1).astype(jnp.bfloat16)

    gathered = gather_all(block, sizes)
    attn = gathered.shape[0]

    tail = gathered[:, :, :, width_local:].astype(jnp.float32)
    summed = jnp.sum(tail[..., : PARTS * STAT], axis=1)
    summed = sum(summed[..., k * STAT : (k + 1) * STAT] for k in range(PARTS))
    scale = lax.rsqrt(summed[..., experts] / features + EPSILON)
    logits = summed[..., :experts] * scale[..., None]
    ids = tail[:, 0, :, PARTS * STAT : PARTS * STAT + 2].astype(jnp.int32)
    choose = ids[..., None] == lax.broadcasted_iota(jnp.int32, (1, 1, 1, experts), 3)
    picked = jnp.sum(jnp.where(choose, logits[:, :, None, :], jnp.float32(0.0)), axis=3)
    first_weight = 1.0 / (1.0 + jnp.exp(picked[..., 1] - picked[..., 0]))
    second_weight = 1.0 / (1.0 + jnp.exp(picked[..., 0] - picked[..., 1]))
    own = lax.axis_index("expert") * local_experts + jnp.arange(local_experts, dtype=jnp.int32)
    mine = ids[:, None, :, :] == own[None, :, None, None]
    hit = jnp.any(mine, axis=3)
    earlier = jnp.tril(jnp.ones((row_count, row_count), jnp.bfloat16), -1)
    before = jnp.einsum(
        "anr,qr->anq", hit.astype(jnp.bfloat16), earlier, preferred_element_type=jnp.float32
    ).astype(jnp.int32)
    match = jnp.logical_and(
        hit[:, :, None, :], before[:, :, None, :] == lax.broadcasted_iota(jnp.int32, (1, 1, cap, 1), 2)
    )
    selector = match.astype(jnp.bfloat16)
    row_weight = jnp.where(mine[..., 0], first_weight[:, None, :], jnp.float32(0.0)) + jnp.where(
        mine[..., 1], second_weight[:, None, :], jnp.float32(0.0)
    )

    def per_slot(values):
        out = jnp.sum(jnp.where(match, values[:, :, None, :], jnp.float32(0.0)), axis=3)
        return jnp.swapaxes(out, 0, 1).reshape(local_experts, attn * cap, 1)

    slot_weight = per_slot(row_weight)
    slot_scale = per_slot(jnp.broadcast_to(scale[:, None, :], row_weight.shape))

    slab_rows = pick_rows(selector, gathered, width_local)
    gate_part = jnp.einsum("end,edf->enf", slab_rows, w_gate, preferred_element_type=jnp.float32) * slot_scale
    up_part = jnp.einsum("end,edf->enf", slab_rows, w_up, preferred_element_type=jnp.float32) * slot_scale
    activation = (jax.nn.silu(gate_part) * up_part * slot_weight).astype(jnp.bfloat16)
    outputs = jnp.einsum("enf,efd->end", activation, w_down, preferred_element_type=jnp.float32).astype(
        jnp.bfloat16
    )
    partial = place_rows(selector, outputs)
    total = reduce_all(partial, sizes)
    return (hidden_state + total).astype(jnp.bfloat16)


def solution(mesh):
    sizes = grid_of(mesh.shape["attn"], mesh.shape["expert"])
    return jax.shard_map(
        functools.partial(on_device, sizes),
        mesh=mesh,
        in_specs=(
            P("attn", "expert"),
            P("attn", "expert"),
            P("attn", "expert", None, None),
            P("attn", "expert", None, None),
            P("attn", "expert"),
            P("attn", "expert"),
            P("attn"),
            P("expert"),
            P("expert", None),
            P("attn", None),
            P("expert", None, "attn"),
            P("expert", None, "attn"),
            P("expert", "attn", None),
        ),
        out_specs=P("attn", "expert"),
        check_vma=False,
    )
```

time: 325 us -> 184 us (0.57)
  waiting for transfers between devices: 220 us -> 0 us
  Pallas kernels: 0 us -> 120 us
  blocking collectives: 20.3 us -> 0 us
  between operations: 13.6 us -> 0.23 us
  starting transfers between devices: 3.72 us -> 0 us
  other arithmetic: 3.66 us -> 7.36 us
  local copies, waits for them, and re-layouts: 7.22 us -> 3.63 us
    pallas_call x0 -> x4, Pallas kernels: none -> 120 us  [the longest x1 62.7 us: reduce_all(): pl.pallas_call(functools.partial(reduce_kernel, sizes), out_shape=jax.Sha...]
    reduce_scatter x1 -> x0, waiting for transfers between devices: 110 us -> none  [on_device(): lax.psum_scatter(jnp.einsum('enf,efd->ned', activation, w_down, preferred...]
    all_gather x1 -> x0, waiting for transfers between devices: 98.8 us -> none  [on_device(): slab_rows = lax.all_gather(outgoing, 'attn', axis=1, tiled=True)]
    psum x2 -> x0, blocking collectives: 12.8 us -> none  [the longest x1 6.93 us: on_device(): lax.psum(jnp.sum(hidden_state * hidden_state, axis=1), 'expert')]
    all_to_all x1 -> x0, waiting for transfers between devices: 11.3 us -> none  [on_device(): lax.all_to_all(expert_result, 'expert', split_axis=2, concat_axis=1, tile...]
    all_gather x1 -> x0, blocking collectives: 7.56 us -> none  [on_device(): whole_rows = lax.all_gather(narrow, 'expert', axis=1, tiled=True)]
    all_to_all x1 -> x0, starting transfers between devices: 3.49 us -> none  [on_device(): lax.all_to_all(expert_result, 'expert', split_axis=2, concat_axis=1, tile...]
    dot_general x5 -> x3, matrix products: 19.3 us -> 17.3 us  [the longest x1 16.7 us: on_device(): jnp.einsum('enf,efd->end', activation, w_down, preferred_element_type=jnp...]
  transfers between devices with their start and end apart: 3 -> 0, of which waited for: 3 -> 0; matrix products, arithmetic and copies ran while one was open for 0% -> 0% of each run, Pallas kernels for 0% -> 0%
where the time goes in v1:
time: 184 us; the launch traced here: 183 us
  Pallas kernels  120 us (65%)
  matrix products  51.1 us (28%)
  other arithmetic  7.36 us (4%)
  local copies, waits for them, and re-layouts  3.63 us (2%)
    pallas_call x1, Pallas kernels, reduce_all(): pl.pallas_call(functools.partial(reduce_kernel, sizes), out_shape=jax.Sha...  62.7 us
    pallas_call x1, Pallas kernels, gather_all(): pl.pallas_call(functools.partial(gather_kernel, sizes), out_shape=jax.Sha...  39.1 us
    dot_general x1, matrix products, on_device(): jnp.einsum('enf,efd->end', activation, w_down, preferred_element_type=jnp...  16.7 us
    dot_general x1, matrix products, on_device(): jnp.einsum('end,edf->enf', slab_rows, w_gate, preferred_element_type=jnp....  13.5 us
    dot_general x1, matrix products, on_device(): jnp.einsum('end,edf->enf', slab_rows, w_up, preferred_element_type=jnp.fl...  11.9 us
    pallas_call x1, Pallas kernels, place_rows(): pl.pallas_call(place_kernel, grid=(attn,), out_shape=jax.ShapeDtypeStruct...  9.56 us
    pallas_call x1, Pallas kernels, pick_rows(): pl.pallas_call(pick_kernel, grid=(attn,), out_shape=jax.ShapeDtypeStruct(...  9.1 us
    dot_general x1, matrix products, on_device(): jnp.einsum('rkgd,rkld->rkgl', queries, key_cache, preferred_element_type=...  4.64 us

profile of v1, /device:TPU:16, one launch (start us, length us, event | category | flops | bytes accessed | tf_op | source)
XLA Modules:
  0.0 182.8 jit_solution(5023232150140387975)
XLA Ops:
  0.0 0.7 convert_convert_fusion
  0.7 0.7 iota_compare_fusion.4
  1.4 0.1 copy.50
  1.6 0.8 reshape.106
  2.3 0.8 reshape.101
  3.1 1.2 reshape.98
  4.3 0.3 fusion.38
  4.6 4.6 %fusion.37 = (f32[64,2,6]{2,1,0:T(2,128)S(1)}, f32[64,2,6,128]{3,2,1,0:T(8,128)S(1)}) fusion(bf16[64,2,6,128]{3,2,1,0:T(8,128)(2,1)S(1)} %reshape.98, bf16[64,2,128,128]{3,2,1,0:T(8,128)(2,1)} %param.15, pred[64,128]{1,0:T(8,128)(4,1)S(1)} %iota_compare_fusion.4), kind=kOutput, calls=%fused_computation.77 | convolution fusion | flops 25459968 | bytes 4795392 | tf_op jit(solution)/shard_map/rkgd,rkld->rkgl/dot_general | solution.py:451
  9.3 3.4 %convolution_add_fusion = f32[64,2,6,128]{3,2,1,0:T(8,128)S(1)} fusion(bf16[64,2,128,128]{3,2,1,0:T(8,128)(2,1)} %param.16, f32[64,2,6,128]{3,2,1,0:T(8,128)S(1)} %get-tuple-element.21, f32[64,2,128]{2,1,0:T(2,128)S(1)} %reshape.101, f32[64,2,6]{2,1,0:T(2,128)S(1)} %get-tuple-element.12, f32[64,2,6]{2,1,0:T(2,128)S(1)} %get-tuple-element.11), kind=kOutput, calls=%fused_computation.2 | convolution fusion | flops 25559040 | bytes 5052416 | tf_op jit(solution)/shard_map/rkgl,rkld->rkgd/dot_general | solution.py:468
  12.9 0.4 fusion.2
  13.3 0.2 multiply_convert_fusion.1
  13.8 0.7 pad_maximum_fusion.x_ref
  14.5 39.1 %gather_all.1.g_ref = bf16[8,4,64,1664]{3,2,1,0:T(8,128)(2,1)} custom-call(bf16[64,1664]{1,0:T(8,128)(2,1)} %pad_maximum_fusion.x_ref), custom_call_target="tpu_custom_call" | custom-call | tf_op jit(solution)/shard_map/gather_all/pallas_call | solution.py:207
  53.5 1.1 slice_convert_fusion
  54.7 0.1 fusion.7
  54.9 0.2 slice_add_fusion
  55.1 0.3 fusion.6
  55.4 0.1 slice_multiply_fusion
  55.5 0.1 copy.56
  55.6 0.1 copy.55
  55.8 0.1 copy.51
  56.0 0.1 fusion.35
  56.1 0.2 convolution_convert_fusion.1
  56.3 0.3 select_reduce_fusion.1
  56.8 0.7 fusion.10.sel_ref
  57.5 9.1 %pick_rows.1 = bf16[2,256,6144]{2,1,0:T(8,128)(2,1)} custom-call(bf16[8,2,32,64]{3,2,1,0:T(8,128)(2,1)} %fusion.10.sel_ref, bf16[8,4,64,1664]{3,2,1,0:T(8,128)(2,1)} %gather_all.1.g_ref), custom_call_target="tpu_custom_call" | custom-call | tf_op jit(solution)/shard_map/pick_rows/pallas_call | solution.py:386
  66.6 13.5 %fusion.39 = f32[2,256,1024]{2,1,0:T(8,128)S(1)} fusion(bf16[2,256,6144]{2,1,0:T(8,128)(2,1)} %pick_rows.1, bf16[2,6144,1024]{2,1,0:T(8,128)(2,1)} %param.23), kind=kOutput, calls=%fused_computation.79 | convolution fusion | flops 6442450944 | bytes 33554432 | tf_op jit(solution)/shard_map/end,edf->enf/dot_general | solution.py:525
  80.1 11.9 %multiply_convert_fusion = bf16[2,256,1024]{2,1,0:T(8,128)(2,1)S(1)} fusion(f32[2,256,1024]{2,1,0:T(8,128)S(1)} %fusion.39, bf16[2,256,6144]{2,1,0:T(8,128)(2,1)S(1)} %copy-done.2, bf16[2,6144,1024]{2,1,0:T(8,128)(2,1)} %param.24, f32[2,256]{1,0:T(2,128)S(1)} %mul.106, f32[2,256]{1,0:T(2,128)S(1)} %mul.98), kind=kOutput, calls=%fused_computation.1 | convolution fusion | flops 6447169536 | bytes 34607104 | tf_op jit(solution)/shard_map/end,edf->enf/dot_general | solution.py:526
  92.1 16.7 %convolution_convert_fusion.y_ref = bf16[2,256,6144]{2,1,0:T(8,128)(2,1)} fusion(bf16[2,256,1024]{2,1,0:T(8,128)(2,1)S(1)} %multiply_convert_fusion, bf16[2,1024,6144]{2,1,0:T(8,128)(2,1)} %param.25), kind=kOutput, calls=%fused_computation | convolution fusion | flops 6445596672 | bytes 32505856 | tf_op jit(solution)/shard_map/enf,efd->end/dot_general | solution.py:528
  108.8 9.6 %place_rows.1.p_ref = bf16[8,64,6144]{2,1,0:T(8,128)(2,1)} custom-call(bf16[8,2,32,64]{3,2,1,0:T(8,128)(2,1)} %fusion.10.sel_ref, bf16[2,256,6144]{2,1,0:T(8,128)(2,1)} %convolution_convert_fusion.y_ref), custom_call_target="tpu_custom_call" | custom-call | tf_op jit(solution)/shard_map/place_rows/pallas_call | solution.py:413
  118.3 62.7 %reduce_all.1 = f32[64,1536]{1,0:T(8,128)} custom-call(bf16[8,64,6144]{2,1,0:T(8,128)(2,1)} %place_rows.1.p_ref), custom_call_target="tpu_custom_call" | custom-call | tf_op jit(solution)/shard_map/reduce_all/pallas_call | solution.py:349
  181.0 1.7 add_convert_fusion
  (28 shorter events, 0.8 us)
Async XLA Ops:
  0.0 12.9 %copy-start = (f32[1536,8]{0,1:T(8,128)S(1)}, f32[1536,8]{0,1:T(8,128)}, u32[]{:S(2)}) copy-start(f32[1536,8]{0,1:T(8,128)} %param.21) | copy-start | bytes 147460
  4.6 8.3 %copy-start.3 = (bf16[64,1536]{1,0:T(8,128)(2,1)S(1)}, bf16[64,1536]{1,0:T(8,128)(2,1)}, u32[]{:S(2)}) copy-start(bf16[64,1536]{1,0:T(8,128)(2,1)} %param.13) | copy-start | bytes 589828
  4.6 8.3 %copy-start.4 = (f32[1536]{0:T(1024)S(1)}, f32[1536]{0:T(1024)}, u32[]{:S(2)}) copy-start(f32[1536]{0:T(1024)} %param.20) | copy-start | bytes 18436
  66.6 13.6 %copy-start.2 = (bf16[2,256,6144]{2,1,0:T(8,128)(2,1)S(1)}, bf16[2,256,6144]{2,1,0:T(8,128)(2,1)}, u32[]{:S(2)}) copy-start(bf16[2,256,6144]{2,1,0:T(8,128)(2,1)} %pick_rows.1) | copy-start | bytes 18874372
  108.8 74.0 %copy-start.1 = (f32[1536,8]{0,1:T(8,128)S(1)}, f32[1536,8]{0,1:T(8,128)}, u32[]{:S(2)}) copy-start(f32[1536,8]{0,1:T(8,128)} %param.21) | copy-start | bytes 147460

commit v2 on v1

--- a/solution.py
+++ b/solution.py
@@ -13,6 +13,7 @@
 CORES = 2
 PARTS = 3
 STAT = 16
+TILE = 256
 MESH = pl.DeviceIdType.MESH
 
 
@@ -119,70 +120,85 @@
         cond = inside if cond is None else jnp.logical_and(cond, inside)
         send(cond, src, block(bz, x, y), z_send.at[step, way], z_recv.at[step, way], me.device(z=to))
 
+    def second(cond, src, dst, h, bz, other):
+        for way in range(2):
+            along(cond, src, dst, h, 1, 0, way, (bz, other))
+
+    def places(step):
+        if step == 0:
+            return [(None, z)]
+        return [(z - step >= 0, z - step), (z + step < nz, z + step)]
+
+    def both(one, two):
+        return two if one is None else jnp.logical_and(one, two)
+
+    def first_arrivals(distance):
+        for step in range(1, max(nx, ny)):
+            for there, bz in places(distance):
+                for h in range(2):
+                    name, p, n = line(h, 0)
+                    if step >= n:
+                        continue
+                    for way in range(2):
+                        q = p - step if way == 0 else p + step
+                        have = both(there, q >= 0 if way == 0 else q < n)
+                        bx, by = (q, y) if name == "x" else (x, q)
+                        dst = block(bz, bx, by)
+                        index = (h, step - 1, way, bz)
+                        pl.when(have)(
+                            functools.partial(await_block, half(dst, h), p1_send.at[index], p1_recv.at[index])
+                        )
+                        if step < n - 1:
+                            along(have, dst, dst, h, 0, step, way, (bz,))
+                        second(have, dst, dst, h, bz, q)
+                        to_sibling(have, dst, bz, bx, by, h)
+
+    def second_arrivals(distance):
+        for step in range(1, max(nx, ny)):
+            for k in range(max(nx, ny)):
+                for there, bz in places(distance):
+                    for h in range(2):
+                        _, first_p, first_n = line(h, 0)
+                        name, p, n = line(h, 1)
+                        if step >= n or k >= first_n:
+                            continue
+                        other = lax.rem(first_p + k, first_n)
+                        for way in range(2):
+                            q = p - step if way == 0 else p + step
+                            have = both(there, q >= 0 if way == 0 else q < n)
+                            bx, by = (q, other) if name == "x" else (other, q)
+                            dst = block(bz, bx, by)
+                            index = (h, step - 1, way, bz, other)
+                            pl.when(have)(
+                                functools.partial(await_block, half(dst, h), p2_send.at[index], p2_recv.at[index])
+                            )
+                            if step < n - 1:
+                                along(have, dst, dst, h, 1, step, way, (bz, other))
+                            to_sibling(have, dst, bz, bx, by, h)
+
     for way in range(2):
         if nz > 1:
             z_hop(None, x_ref, z, 0, way)
     spread(None, x_ref, z)
+    for h in range(2):
+        second(None, x_ref, block(z, x, y), h, z, line(h, 0)[1])
     local = pltpu.make_async_copy(x_ref, block(z, x, y), local_sem)
     local.start()
-    for step in range(1, nz):
-        for way in range(2):
-            bz = z - step if way == 0 else z + step
-            have = bz >= 0 if way == 0 else bz < nz
-            dst = block(bz, x, y)
-            pl.when(have)(functools.partial(await_block, dst, z_send.at[step - 1, way], z_recv.at[step - 1, way]))
-            if step < nz - 1:
-                z_hop(have, dst, bz, step, way)
-            spread(have, dst, bz)
-    turn = jnp.where(z < nz // 2, 1, nz - 1)
-    order = [lax.rem(z + k * turn, nz) for k in range(nz)]
-
-    def second(cond, src, h, bz, other):
-        for way in range(2):
-            along(cond, src, src, h, 1, 0, way, (bz, other))
-
+    for step in range(1, nz + 2):
+        if step < nz:
+            for way, (have, bz) in enumerate(places(step)):
+                dst = block(bz, x, y)
+                pl.when(have)(functools.partial(await_block, dst, z_send.at[step - 1, way], z_recv.at[step - 1, way]))
+                if step < nz - 1:
+                    z_hop(have, dst, bz, step, way)
+                spread(have, dst, bz)
+                for h in range(2):
+                    second(have, dst, dst, h, bz, line(h, 0)[1])
+        if step <= nz:
+            first_arrivals(step - 1)
+        if step >= 2:
+            second_arrivals(step - 2)
     local.wait()
-    for bz in order:
-        for h in range(2):
-            second(None, block(bz, x, y), h, bz, line(h, 0)[1])
-    for step in range(1, max(nx, ny)):
-        for bz in order:
-            for h in range(2):
-                name, p, n = line(h, 0)
-                if step >= n:
-                    continue
-                for way in range(2):
-                    q = p - step if way == 0 else p + step
-                    have = q >= 0 if way == 0 else q < n
-                    bx, by = (q, y) if name == "x" else (x, q)
-                    dst = block(bz, bx, by)
-                    index = (h, step - 1, way, bz)
-                    pl.when(have)(functools.partial(await_block, half(dst, h), p1_send.at[index], p1_recv.at[index]))
-                    if step < n - 1:
-                        along(have, dst, dst, h, 0, step, way, (bz,))
-                    second(have, dst, h, bz, q)
-                    to_sibling(have, dst, bz, bx, by, h)
-    for step in range(1, max(nx, ny)):
-        for k in range(max(nx, ny)):
-            for bz in order:
-                for h in range(2):
-                    _, first_p, first_n = line(h, 0)
-                    name, p, n = line(h, 1)
-                    if step >= n or k >= first_n:
-                        continue
-                    other = lax.rem(first_p + k, first_n)
-                    for way in range(2):
-                        q = p - step if way == 0 else p + step
-                        have = q >= 0 if way == 0 else q < n
-                        bx, by = (q, other) if name == "x" else (other, q)
-                        dst = block(bz, bx, by)
-                        index = (h, step - 1, way, bz, other)
-                        pl.when(have)(
-                            functools.partial(await_block, half(dst, h), p2_send.at[index], p2_recv.at[index])
-                        )
-                        if step < n - 1:
-                            along(have, dst, dst, h, 1, step, way, (bz, other))
-                        to_sibling(have, dst, bz, bx, by, h)
     for bz in range(nz):
         for bx in range(nx):
             for by in range(ny):
@@ -216,7 +232,27 @@
 
 
 def reduce_kernel(
-    sizes, p_ref, o_ref, acc, sib, r1, r2, r3, s_send, s_recv, c1_send, c1_recv, c2_send, c2_recv, c3_send, c3_recv
+    sizes,
+    act_ref,
+    sel_ref,
+    w_ref,
+    o_ref,
+    p_ref,
+    w_buf,
+    acc,
+    sib,
+    r1,
+    r2,
+    r3,
+    w_sem,
+    s_send,
+    s_recv,
+    c1_send,
+    c1_recv,
+    c2_send,
+    c2_recv,
+    c3_send,
+    c3_recv,
 ):
     me = Place(sizes)
     nz, nx, ny = sizes
@@ -224,7 +260,11 @@
     width = o_ref.shape[1]
     cols = halves_of(width)
     whole = (pl.ds(0, width),)
-    me.greet()
+    local = act_ref.shape[0]
+    groups, group_rows, deep = sel_ref.shape
+    slots = deep // local
+    per_group = group_rows // p_ref.shape[1]
+    tile = math.gcd(width, TILE)
     started = []
 
     def remote(src, dst, ssem, rsem, dev):
@@ -235,14 +275,47 @@
     def part(by, core):
         return pl.ds(pl.multiple_of((by * CORES + core) * width, LANES), width)
 
-    blocks = [(bz, bx, by) for bz in range(nz) for bx in range(nx) for by in range(ny)]
-    for bz, bx, by in blocks:
-        a = bz * nx + bx
-        copy = remote(
-            p_ref.at[a, :, part(by, 1 - c)], sib.at[a, by], s_send.at[a, by], s_recv.at[a, by], me.device(c=1 - c)
-        )
-        copy.start()
-        started.append((None, copy))
+    chunks = [(by, core) for core in (1 - c, c) for by in range(ny)]
+    loads = []
+    for k, (by, core) in enumerate(chunks):
+        load = pltpu.make_async_copy(w_ref.at[:, :, part(by, core)], w_buf.at[k], w_sem.at[k])
+        load.start()
+        loads.append(load)
+    me.greet()
+
+    def project(k, by, core):
+        base = (by * CORES + core) * width
+
+        def one(t, carry):
+            offset = pl.multiple_of(t * tile, tile)
+            place = pl.ds(pl.multiple_of(base + offset, LANES), tile)
+            outs = [
+                jnp.dot(
+                    act_ref[n], w_buf[k, n, :, pl.ds(offset, tile)], preferred_element_type=jnp.float32
+                ).astype(p_ref.dtype)
+                for n in range(local)
+            ]
+            for g in range(groups):
+                mixed = [out[g * slots : (g + 1) * slots] for out in outs]
+                mixed = mixed[0] if local == 1 else jnp.concatenate(mixed, axis=0)
+                rows = jnp.dot(sel_ref[g], mixed, preferred_element_type=jnp.float32).astype(p_ref.dtype)
+                for i in range(per_group):
+                    p_ref[g * per_group + i, :, place] = rows[i * p_ref.shape[1] : (i + 1) * p_ref.shape[1]]
+            return carry
+
+        lax.fori_loop(0, width // tile, one, 0)
+
+    for k, (by, core) in enumerate(chunks):
+        loads[k].wait()
+        project(k, by, core)
+        if k < ny:
+            for a in range(nz * nx):
+                copy = remote(
+                    p_ref.at[a, :, part(by, 1 - c)], sib.at[a, by], s_send.at[a, by], s_recv.at[a, by],
+                    me.device(c=1 - c),
+                )
+                copy.start()
+                started.append((None, copy))
 
     def add(view, col, from_ref):
         view[:, col] = (view[:, col].astype(jnp.float32) + from_ref[:, col].astype(jnp.float32)).astype(view.dtype)
@@ -288,32 +361,45 @@
         return [r2.at[way, k] for way in range(2)], c2_send.at[h, k], c2_recv.at[h, k]
 
     at = {"x": x, "y": y}
-    for bz, bx, by in blocks:
-        a = bz * nx + bx
-        remote(sib.at[a, by], sib.at[a, by], s_send.at[a, by], s_recv.at[a, by], me.device(c=1 - c)).wait_recv()
-        acc[a, by] = (
-            p_ref[a, :, part(by, c)].astype(jnp.float32) + sib[a, by].astype(jnp.float32)
-        ).astype(acc.dtype)
-        for h in range(2):
-            (name, target), _ = lines(h, bx, by)
-            chain(acc.at[a, by], cols[h], name, target, *first_args(h, a, by))
-    for bz, bx, by in blocks:
-        a = bz * nx + bx
-        for h in range(2):
-            (name, target), (name2, target2) = lines(h, bx, by)
-            here = at[name] == target
-            finish(here, acc.at[a, by], cols[h], name, *first_args(h, a, by))
-            chain(acc.at[a, by], cols[h], name2, target2, *second_args(h, bz, bx, by), here=here)
-    for bz, bx, by in blocks:
-        a = bz * nx + bx
-        here = jnp.logical_and(x == bx, y == by)
-        for h in range(2):
-            _, (name2, target2) = lines(h, bx, by)
-            finish(here, acc.at[a, by], cols[h], name2, *second_args(h, bz, bx, by))
-    for bz in sorted(range(nz), key=lambda place: min(place, nz - 1 - place)):
-        view = acc.at[bz * nx + x, y]
+    plane = [(bx, by) for bx in range(nx) for by in range(ny)]
+
+    def begin(bz):
+        for bx, by in plane:
+            a = bz * nx + bx
+            remote(sib.at[a, by], sib.at[a, by], s_send.at[a, by], s_recv.at[a, by], me.device(c=1 - c)).wait_recv()
+            acc[a, by] = (
+                p_ref[a, :, part(by, c)].astype(jnp.float32) + sib[a, by].astype(jnp.float32)
+            ).astype(acc.dtype)
+            for h in range(2):
+                (name, target), _ = lines(h, bx, by)
+                chain(acc.at[a, by], cols[h], name, target, *first_args(h, a, by))
+
+    def go_on(bz):
+        for bx, by in plane:
+            a = bz * nx + bx
+            for h in range(2):
+                (name, target), (name2, target2) = lines(h, bx, by)
+                here = at[name] == target
+                finish(here, acc.at[a, by], cols[h], name, *first_args(h, a, by))
+                chain(acc.at[a, by], cols[h], name2, target2, *second_args(h, bz, bx, by), here=here)
+
+    def to_z(bz):
+        for bx, by in plane:
+            here = jnp.logical_and(x == bx, y == by)
+            for h in range(2):
+                _, (name2, _) = lines(h, bx, by)
+                finish(here, acc.at[bz * nx + bx, by], cols[h], name2, *second_args(h, bz, bx, by))
         landing = [r3.at[way, bz] for way in range(2)]
-        chain(view, whole[0], "z", bz, landing, c3_send.at[bz], c3_recv.at[bz])
+        chain(acc.at[bz * nx + x, y], whole[0], "z", bz, landing, c3_send.at[bz], c3_recv.at[bz])
+
+    order = sorted(range(nz), key=lambda place: min(place, nz - 1 - place))
+    for k in range(nz + 2):
+        if k < nz:
+            begin(order[k])
+        if 1 <= k <= nz:
+            go_on(order[k - 1])
+        if k >= 2:
+            to_z(order[k - 2])
     for bz in range(nz):
         landing = [r3.at[way, bz] for way in range(2)]
 
@@ -339,24 +425,29 @@
             pl.when(cond)(copy.wait_send)
 
 
-def reduce_all(partial, sizes):
+def reduce_all(activation, selector, w_down, sizes):
     nz, nx, ny = sizes
-    attn, rows, full = partial.shape
+    local, depth, full = w_down.shape
+    attn = nz * nx
+    rows = selector.shape[0] * selector.shape[1] // attn
     width = full // (ny * CORES)
     wide = max(nx, ny)
     dma = pltpu.SemaphoreType.DMA
-    kind = partial.dtype
+    kind = activation.dtype
     return pl.pallas_call(
         functools.partial(reduce_kernel, sizes),
         out_shape=jax.ShapeDtypeStruct((rows, width), jnp.float32),
-        in_specs=[pl.BlockSpec(memory_space=pltpu.VMEM)],
+        in_specs=[pl.BlockSpec(memory_space=pltpu.VMEM)] * 2 + [pl.BlockSpec(memory_space=pl.ANY)],
         out_specs=pl.BlockSpec(memory_space=pltpu.VMEM),
         scratch_shapes=[
+            pltpu.VMEM((attn, rows, full), kind),
+            pltpu.VMEM((ny * CORES, local, depth, width), kind),
             pltpu.VMEM((attn, ny, rows, width), kind),
             pltpu.VMEM((attn, ny, rows, width), kind),
             pltpu.VMEM((2, attn, ny, rows, width), kind),
             pltpu.VMEM((2, nz * wide, rows, width), kind),
             pltpu.VMEM((2, nz, rows, width), kind),
+            dma((ny * CORES,)),
         ]
         + [dma((attn, ny))] * 2
         + [dma((2, attn, ny, 2))] * 2
@@ -366,61 +457,37 @@
             collective_id=1, has_side_effects=True, vmem_limit_bytes=60 * 2**20
         ),
         name="reduce_all",
-    )(partial)
+    )(activation, selector, w_down)
 
 
 def pick_kernel(sel_ref, g_ref, out_ref):
-    local, cap, rows = sel_ref.shape[1:]
-    devices = g_ref.shape[1]
-    width = out_ref.shape[2] // devices
-    chosen = sel_ref[0].reshape(local * cap, rows)
-    for e in range(devices):
-        taken = jnp.dot(chosen, g_ref[0, e, :, :width], preferred_element_type=jnp.float32)
-        taken = taken.astype(out_ref.dtype).reshape(local, cap, width)
-        out_ref[:, :, e * width : (e + 1) * width] = taken
-
-
-def pick_rows(selector, gathered, width):
-    attn, local, cap, rows = selector.shape
-    devices, full = gathered.shape[1], gathered.shape[3]
+    local, slots, width = out_ref.shape
+    rows = sel_ref.shape[1]
+    taken = lax.dot_general(
+        sel_ref[0],
+        g_ref[:, 0, :, :width].reshape(rows, width),
+        (((0,), (0,)), ((), ())),
+        preferred_element_type=jnp.float32,
+    )
+    out_ref[...] = taken.astype(out_ref.dtype).reshape(local, slots, width)
+
+
+def pick_rows(selector, gathered, width, local):
+    groups, group_rows, deep = selector.shape
+    attn, devices, rows, full = gathered.shape
+    per_group = attn // groups
+    slots = deep // local
     return pl.pallas_call(
         pick_kernel,
-        grid=(attn,),
-        out_shape=jax.ShapeDtypeStruct((local, attn * cap, devices * width), gathered.dtype),
+        grid=(groups, devices),
+        out_shape=jax.ShapeDtypeStruct((local, groups * slots, devices * width), gathered.dtype),
         in_specs=[
-            pl.BlockSpec((1, local, cap, rows), lambda a: (a, 0, 0, 0)),
-            pl.BlockSpec((1, devices, rows, full), lambda a: (a, 0, 0, 0)),
+            pl.BlockSpec((1, group_rows, deep), lambda g, e: (g, 0, 0)),
+            pl.BlockSpec((per_group, 1, rows, full), lambda g, e: (g, e, 0, 0)),
         ],
-        out_specs=pl.BlockSpec((local, cap, devices * width), lambda a: (0, a, 0)),
+        out_specs=pl.BlockSpec((local, slots, width), lambda g, e: (0, g, e)),
         name="pick_rows",
     )(selector, gathered)
-
-
-def place_kernel(sel_ref, y_ref, out_ref):
-    local = sel_ref.shape[1]
-    total = None
-    for n in range(local):
-        term = lax.dot_general(
-            sel_ref[0, n], y_ref[n], (((0,), (0,)), ((), ())), preferred_element_type=jnp.float32
-        )
-        total = term if total is None else total + term
-    out_ref[0] = total.astype(out_ref.dtype)
-
-
-def place_rows(selector, outputs):
-    attn, local, cap, rows = selector.shape
-    full = outputs.shape[2]
-    return pl.pallas_call(
-        place_kernel,
-        grid=(attn,),
-        out_shape=jax.ShapeDtypeStruct((attn, rows, full), jnp.bfloat16),
-        in_specs=[
-            pl.BlockSpec((1, local, cap, rows), lambda a: (a, 0, 0, 0)),
-            pl.BlockSpec((local, cap, full), lambda a: (0, a, 0)),
-        ],
-        out_specs=pl.BlockSpec((1, rows, full), lambda a: (a, 0, 0)),
-        name="place_rows",
-    )(selector, outputs)
 
 
 def on_device(
@@ -509,7 +576,13 @@
     match = jnp.logical_and(
         hit[:, :, None, :], before[:, :, None, :] == lax.broadcasted_iota(jnp.int32, (1, 1, cap, 1), 2)
     )
-    selector = match.astype(jnp.bfloat16)
+    per_group = math.gcd(attn, max(TILE // row_count, 1))
+    split = match.reshape(attn // per_group, per_group, local_experts, cap, row_count)
+    same = jnp.eye(per_group, dtype=bool)
+    selector = jnp.logical_and(
+        jnp.transpose(split, (0, 1, 4, 2, 3))[:, :, :, :, None, :], same[None, :, None, None, :, None]
+    )
+    selector = selector.reshape(attn // per_group, per_group * row_count, -1).astype(jnp.bfloat16)
     row_weight = jnp.where(mine[..., 0], first_weight[:, None, :], jnp.float32(0.0)) + jnp.where(
         mine[..., 1], second_weight[:, None, :], jnp.float32(0.0)
     )
@@ -521,15 +594,11 @@
     slot_weight = per_slot(row_weight)
     slot_scale = per_slot(jnp.broadcast_to(scale[:, None, :], row_weight.shape))
 
-    slab_rows = pick_rows(selector, gathered, width_local)
+    slab_rows = pick_rows(selector, gathered, width_local, local_experts)
     gate_part = jnp.einsum("end,edf->enf", slab_rows, w_gate, preferred_element_type=jnp.float32) * slot_scale
     up_part = jnp.einsum("end,edf->enf", slab_rows, w_up, preferred_element_type=jnp.float32) * slot_scale
     activation = (jax.nn.silu(gate_part) * up_part * slot_weight).astype(jnp.bfloat16)
-    outputs = jnp.einsum("enf,efd->end", activation, w_down, preferred_element_type=jnp.float32).astype(
-        jnp.bfloat16
-    )
-    partial = place_rows(selector, outputs)
-    total = reduce_all(partial, sizes)
+    total = reduce_all(activation, selector, w_down, sizes)
     return (hidden_state + total).astype(jnp.bfloat16)
 
 

time: 184 us -> 159 us (0.86)
  matrix products: 51.1 us -> 33.2 us
  Pallas kernels: 120 us -> 112 us
    dot_general x1 -> x0, matrix products: 16.7 us -> none  [on_device(): jnp.einsum('enf,efd->end', activation, w_down, preferred_element_type=jnp...]
    pallas_call x2 -> x1, Pallas kernels: 18.7 us -> 9.4 us  [pick_rows(): pl.pallas_call(pick_kernel, grid=(groups, devices), out_shape=jax.ShapeDt...]
    pallas_call x1, Pallas kernels: 62.7 us -> 66.2 us  [reduce_all(): pl.pallas_call(functools.partial(reduce_kernel, sizes), out_shape=jax.Sha...]
    pallas_call x1, Pallas kernels: 39.1 us -> 36.2 us  [gather_all(): pl.pallas_call(functools.partial(gather_kernel, sizes), out_shape=jax.Sha...]
    dot_general x1, matrix products: 3.45 us -> 1.27 us  [on_device(): jnp.einsum('rkgl,rkld->rkgd', weights_cache, value_cache, preferred_eleme...]
where the time goes in v2:
time: 159 us; the launch traced here: 158 us
  Pallas kernels  112 us (70%)
  matrix products  33.2 us (21%)
  other arithmetic  7.53 us (5%)
  local copies, waits for them, and re-layouts  5.16 us (3%)
    pallas_call x1, Pallas kernels, reduce_all(): pl.pallas_call(functools.partial(reduce_kernel, sizes), out_shape=jax.Sha...  66.2 us
    pallas_call x1, Pallas kernels, gather_all(): pl.pallas_call(functools.partial(gather_kernel, sizes), out_shape=jax.Sha...  36.2 us
    dot_general x1, matrix products, on_device(): jnp.einsum('end,edf->enf', slab_rows, w_gate, preferred_element_type=jnp....  13.5 us
    dot_general x1, matrix products, on_device(): jnp.einsum('end,edf->enf', slab_rows, w_up, preferred_element_type=jnp.fl...  12.7 us
    pallas_call x1, Pallas kernels, pick_rows(): pl.pallas_call(pick_kernel, grid=(groups, devices), out_shape=jax.ShapeDt...  9.4 us
    dot_general x1, matrix products, on_device(): jnp.einsum('rkgd,rkld->rkgl', queries, key_cache, preferred_element_type=...  4.75 us

profile of v2, /device:TPU:16, one launch (start us, length us, event | category | flops | bytes accessed | tf_op | source)
XLA Modules:
  0.0 157.9 jit_solution(13745924088674859560)
XLA Ops:
  0.0 0.7 convert_convert_fusion
  0.7 0.7 iota_compare_fusion.5
  1.6 0.8 reshape.122
  2.3 0.8 reshape.117
  3.1 0.1 and.45
  3.3 0.2 and.46
  3.5 0.2 copy.87
  3.7 1.2 reshape.114
  4.9 0.3 fusion.34
  5.2 4.8 %fusion.33 = (f32[64,2,6]{2,1,0:T(2,128)S(1)}, f32[64,2,6,128]{3,2,1,0:T(8,128)S(1)}) fusion(bf16[64,2,6,128]{3,2,1,0:T(8,128)(2,1)S(1)} %reshape.114, bf16[64,2,128,128]{3,2,1,0:T(8,128)(2,1)} %param.15, pred[64,128]{1,0:T(8,128)(4,1)S(1)} %iota_compare_fusion.5), kind=kOutput, calls=%fused_computation.76 | convolution fusion | flops 25459968 | bytes 4795392 | tf_op jit(solution)/shard_map/rkgd,rkld->rkgl/dot_general | solution.py:518
  10.1 1.3 convolution_add_fusion
  11.5 0.4 fusion.2
  11.9 0.2 multiply_convert_fusion.1
  12.3 0.7 pad_maximum_fusion.x_ref
  13.0 36.2 %gather_all.1.g_ref = bf16[8,4,64,1664]{3,2,1,0:T(8,128)(2,1)} custom-call(bf16[64,1664]{1,0:T(8,128)(2,1)} %pad_maximum_fusion.x_ref), custom_call_target="tpu_custom_call" | custom-call | tf_op jit(solution)/shard_map/gather_all/pallas_call | solution.py:223
  49.2 1.1 slice_convert_fusion
  50.4 0.1 fusion.7
  50.6 0.2 slice_add_fusion
  50.8 0.3 fusion.6
  51.4 0.1 copy.92
  51.5 0.1 copy.84
  51.8 0.2 convolution_convert_fusion
  52.0 0.3 select_reduce_fusion.1
  52.6 0.2 and.43
  52.8 0.5 and.44
  53.3 0.3 copy.88
  53.6 0.8 and_convert_fusion.sel_ref
  54.4 9.4 %pick_rows.1 = bf16[2,256,6144]{2,1,0:T(8,128)(2,1)} custom-call(bf16[2,256,256]{2,1,0:T(8,128)(2,1)} %and_convert_fusion.sel_ref, bf16[8,4,64,1664]{3,2,1,0:T(8,128)(2,1)} %gather_all.1.g_ref), custom_call_target="tpu_custom_call" | custom-call | tf_op jit(solution)/shard_map/pick_rows/pallas_call | solution.py:480
  63.8 13.5 %fusion.35 = f32[2,256,1024]{2,1,0:T(8,128)S(1)} fusion(bf16[2,256,6144]{2,1,0:T(8,128)(2,1)} %pick_rows.1, bf16[2,6144,1024]{2,1,0:T(8,128)(2,1)} %param.23), kind=kOutput, calls=%fused_computation.78 | convolution fusion | flops 6442450944 | bytes 33554432 | tf_op jit(solution)/shard_map/end,edf->enf/dot_general | solution.py:598
  77.3 12.7 %multiply_convert_fusion.act_ref = bf16[2,256,1024]{2,1,0:T(8,128)(2,1)} fusion(f32[2,256,1024]{2,1,0:T(8,128)S(1)} %fusion.35, bf16[2,256,6144]{2,1,0:T(8,128)(2,1)S(1)} %copy-done.2, bf16[2,6144,1024]{2,1,0:T(8,128)(2,1)} %param.24, f32[2,256]{1,0:T(2,128)S(1)} %mul.106, f32[2,256]{1,0:T(2,128)S(1)} %mul.98), kind=kOutput, calls=%fused_computation | convolution fusion | flops 6447169536 | bytes 34607104 | tf_op jit(solution)/shard_map/end,edf->enf/dot_general | solution.py:599
  90.0 66.2 %reduce_all.1 = f32[64,1536]{1,0:T(8,128)} custom-call(bf16[2,256,1024]{2,1,0:T(8,128)(2,1)} %multiply_convert_fusion.act_ref, bf16[2,256,256]{2,1,0:T(8,128)(2,1)} %and_convert_fusion.sel_ref, bf16[2,1024,6144]{2,1,0:T(8,128)(2,1)} %w_ref.1), custom_call_target="tpu_custom_call" | custom-call | tf_op jit(solution)/shard_map/reduce_all/pallas_call | solution.py:437
  156.2 1.7 %add_convert_fusion = bf16[64,1536]{1,0:T(8,128)(2,1)} fusion(f32[64,1536]{1,0:T(8,128)} %reduce_all.1, f32[64,1536]{1,0:T(8,128)S(1)} %reshape.116, bf16[64,1536]{1,0:T(8,128)(2,1)S(1)} %copy-done.3), kind=kLoop, calls=%fused_computation.10 | loop fusion | flops 393216 | bytes 1179648 | tf_op jit(solution)/shard_map/convert_element_type | solution.py:602
  (38 shorter events, 1.3 us)
Async XLA Ops:
  0.0 11.4 %copy-start = (f32[1536,8]{0,1:T(8,128)S(1)}, f32[1536,8]{0,1:T(8,128)}, u32[]{:S(2)}) copy-start(f32[1536,8]{0,1:T(8,128)} %param.21) | copy-start | bytes 147460
  4.9 5.1 %copy-start.5 = (bf16[64,2,128,128]{3,2,1,0:T(8,128)(2,1)S(1)}, bf16[64,2,128,128]{3,2,1,0:T(8,128)(2,1)}, u32[]{:S(2)}) copy-start(bf16[64,2,128,128]{3,2,1,0:T(8,128)(2,1)} %param.16) | copy-start | bytes 12582916
  10.0 1.4 copy-start.3
  10.0 1.4 copy-start.4
  63.7 13.6 %copy-start.2 = (bf16[2,256,6144]{2,1,0:T(8,128)(2,1)S(1)}, bf16[2,256,6144]{2,1,0:T(8,128)(2,1)}, u32[]{:S(2)}) copy-start(bf16[2,256,6144]{2,1,0:T(8,128)(2,1)} %pick_rows.1) | copy-start | bytes 18874372
  90.0 67.9 %copy-start.1 = (f32[1536,8]{0,1:T(8,128)S(1)}, f32[1536,8]{0,1:T(8,128)}, u32[]{:S(2)}) copy-start(f32[1536,8]{0,1:T(8,128)} %param.21) | copy-start | bytes 147460
